TPU v7x, 32 devices: a whole 2x2x4 slice. The times are simulated.
32 devices in a mesh: state: 4 (over z), basis: 8 (over y, x, core).
Axes of the slice: x: 2, y: 2, z: 4, core: 2. Of those that a mesh axis runs over, the one named last changes fastest.
Arguments:
- states: float32 [8, 64, 64000], P('state', 'basis'), may hold values from -40 to 40
- membrane_step: float32 [40, 40], replicated, may hold values from -1 to 1
- cavity_forward: float32 [64, 64], replicated, may hold values from -0.75 to 0.75
- coupling: float32 [64, 40], replicated, may hold values from 0.25 to 1
- membrane_forward: float32 [40, 40], replicated, may hold values from -1 to 1
- cavity_back: float32 [64, 64], replicated, may hold values from -9 to 9
- membrane_back: float32 [40, 40], replicated, may hold values from -1 to 1
Outputs:
- orthonormal: float32 [8, 64, 64000], P('state', 'basis')
All inputs are finite; a program needn't handle non-finite values.
Results may differ from a plain program's by a relative error of at most 0.000075.
Values sent between devices are 32-bit elements; how exact they have to be, the bound alone decides.
A program may use at most 192 MiB of HBM per device.

v0:
```python
import jax
import jax.numpy as jnp
from jax import lax
from jax.sharding import PartitionSpec as P


def body(
    states, membrane_step, cavity_forward, coupling, membrane_forward, cavity_back, membrane_back
):
    highest = lax.Precision.HIGHEST
    panel_size, level_count, joint = states.shape
    levels_all = cavity_forward.shape[0]
    membrane_levels = membrane_step.shape[0]
    basis_total = float(levels_all * joint)
    head = jnp.einsum(
        "ab,scbr->scar",
        membrane_step,
        states.reshape(panel_size, level_count, membrane_levels, joint // membrane_levels),
        precision=highest,
    )
    head = head.reshape(panel_size, level_count, joint)
    panel_block = lax.all_to_all(head, "basis", split_axis=2, concat_axis=1, tiled=True)
    items, cavity_all, columns = panel_block.shape
    grid = jnp.einsum("qc,kcr->kqr", cavity_forward, panel_block, precision=highest)
    grid = jnp.einsum(
        "kqtm,nm->kqtn",
        grid.reshape(items, cavity_all, columns // membrane_levels, membrane_levels),
        membrane_forward,
        precision=highest,
    )
    weighted = grid * coupling[None, :, None, :]
    backward = jnp.einsum("kqtn,mn->kqtm", weighted, membrane_back, precision=highest)
    backward = backward.reshape(items, cavity_all, columns)
    stepped = jnp.einsum("cq,kqr->kcr", cavity_back, backward, precision=highest)
    spread = lax.all_to_all(stepped, "state", split_axis=2, concat_axis=0, tiled=True)
    state_total, spread_levels, spread_cols = spread.shape
    flattened = spread.reshape(state_total, -1)
    partial_gram = jnp.dot(flattened, flattened.T, precision=highest)
    gram = lax.psum(partial_gram, ("state", "basis")) / basis_total
    lower_factor = jnp.linalg.cholesky(gram)
    identity = jnp.eye(state_total, dtype=gram.dtype)
    inverse = lax.linalg.triangular_solve(lower_factor, identity, left_side=True, lower=True)
    local_result = jnp.dot(inverse, flattened, precision=highest)
    local_result = local_result.reshape(state_total, spread_levels, spread_cols)
    return lax.all_to_all(
        lax.all_to_all(local_result, "state", split_axis=0, concat_axis=2, tiled=True),
        "basis",
        split_axis=1,
        concat_axis=2,
        tiled=True,
    )


def solution(mesh):
    in_specs = (P("state", "basis", None), P(), P(), P(), P(), P(), P())
    out_specs = P("state", "basis", None)
    return jax.shard_map(body, mesh=mesh, in_specs=in_specs, out_specs=out_specs, check_vma=False)
```

profile of v0, /device:TPU:0, one launch (start us, length us, event | category | flops | bytes accessed | tf_op | source)
XLA Modules:
  0.0 946.3 jit_solution(17978958401633566701)
XLA Ops:
  0.0 0.0 copy-start
  0.0 0.0 copy-start.3
  0.0 4.5 reshape.28
  4.5 0.0 copy-done.3
  4.5 8.0 convolution_bitcast_fusion.2
  12.4 49.2 %copy.60 = f32[2,8,40,1600]{1,0,3,2:T(2,128)} copy(f32[2,8,40,1600]{3,2,1,0:T(8,128)} %convolution_bitcast_fusion.2) | data formatting | bytes 8192000 | tf_op jit(solution)/shard_map/reshape | solution.py:21
  61.6 137.2 %reshape.39 = f32[8,1,128000]{2,1,0:T(1,128)} reshape(f32[64000,2,8]{2,1,0:T(2,128)} %bitcast.76) | data formatting | bytes 8192000
  198.8 0.0 copy-start.6
  198.8 5.3 all-to-all-start
  204.1 0.0 copy-done.6
  204.1 0.1 copy.41
  204.2 48.1 %all-to-all-done = f32[8,1,128000]{2,1,0:T(1,128)} async-done(((f32[8,1,128000]{2,1,0:T(1,128)}), f32[8,1,128000]{2,1,0:T(1,128)}, u32[]{:S(2)}, u32[]{:S(2)}) %all-to-all-start) | async-done | bytes 4096032 | tf_op jit(solution)/shard_map/all_to_all | solution.py:22
  252.2 0.5 broadcast.49
  252.8 13.6 %reduce.6 = f32[8,128000]{1,0:T(8,128)} reduce(f32[8,1,128000]{2,1,0:T(1,128)} %all-to-all-done, f32[]{:T(128)} %broadcast.49), dimensions={1}, to_apply=%all_to_all.50.reduce_sub_computation | reduce | bytes 8192004 | tf_op jit(solution)/shard_map/all_to_all | solution.py:22
  266.4 142.2 %reshape.40 = f32[64000,2,8]{2,1,0:T(2,128)} reshape(f32[8,128000]{1,0:T(8,128)} %reduce.6) | data formatting | bytes 8192000
  408.6 71.1 %copy.38 = f32[2,8,8,8000]{3,1,2,0:T(8,128)} copy(f32[2,8,8,8000]{1,0,3,2:T(2,128)} %bitcast.77) | data formatting | bytes 8192000 | tf_op jit(solution)/shard_map/all_to_all | solution.py:22
  479.7 0.0 copy-done
  479.7 8.0 convolution_bitcast_fusion.1
  487.7 6.8 copy.39
  494.5 0.0 copy-start.4
  494.5 8.8 copy.40
  503.3 0.0 copy-done.4
  503.3 0.0 copy-start.5
  503.3 6.5 fusion.9
  509.8 0.0 copy-done.5
  509.8 7.1 fusion
  517.0 0.0 copy-start.2
  517.0 8.2 copy.42
  525.2 0.0 copy-done.2
  525.2 13.7 %convolution_bitcast_fusion = f32[2,64,8000]{2,1,0:T(8,128)} fusion(f32[2,64,8000]{1,2,0:T(8,128)} %bitcast.78, f32[64,64]{1,0:T(8,128)S(1)} %copy-done.2), kind=kOutput, calls=%fused_computation | convolution fusion | flops 786432000 | bytes 8208384 | tf_op jit(solution)/shard_map/cq,kqr->kcr/dot_general | solution.py:34
  538.9 10.7 %copy.44 = f32[2,64,8000]{1,0,2:T(2,128)} copy(f32[2,64,8000]{2,1,0:T(8,128)} %convolution_bitcast_fusion) | data formatting | bytes 8192000 | tf_op jit(solution)/shard_map/cq,kqr->kcr/transpose | solution.py:34
  549.6 11.3 %reshape.41 = f32[4,1,256000]{2,1,0:T(1,128)} reshape(f32[8000,2,64]{2,1,0:T(2,128)} %bitcast.81) | data formatting | bytes 8192000
  560.9 94.7 %all_to_all.69 = f32[4,1,256000]{2,1,0:T(1,128)} all-to-all(f32[4,1,256000]{2,1,0:T(1,128)} %reshape.41), channel_id=1, replica_groups=mesh['state'=4,'basis'=8] {'state'}, dimensions={0} | all-to-all | bytes 8192000 | tf_op jit(solution)/shard_map/all_to_all | solution.py:35
  655.6 14.4 %reduce.7 = f32[4,256000]{1,0:T(4,128)} reduce(f32[4,1,256000]{2,1,0:T(1,128)} %all_to_all.69, f32[]{:T(128)} %broadcast.49), dimensions={1}, to_apply=%all_to_all.54.reduce_sub_computation | reduce | bytes 8192004 | tf_op jit(solution)/shard_map/all_to_all | solution.py:35
  670.0 11.7 %reshape.42 = f32[8000,2,64]{2,1,0:T(2,128)} reshape(f32[4,256000]{1,0:T(4,128)} %reduce.7) | data formatting | bytes 8192000
  681.8 12.6 %copy.45 = f32[2,64,4,2000]{3,1,0,2:T(8,128)} copy(f32[2,64,4,2000]{1,0,3,2:T(2,128)} %bitcast.82) | data formatting | bytes 8192000 | tf_op jit(solution)/shard_map/all_to_all | solution.py:35
  694.3 7.5 reshape.32
  701.8 12.3 %fusion.15 = f32[8,8]{0,1:T(8,128)S(1)} fusion(f32[8,128000]{1,0:T(8,128)} %reshape.32), kind=kOutput, calls=%fused_computation.28 | convolution fusion | flops 98304000 | bytes 4096256 | tf_op jit(solution)/shard_map/dot_general | solution.py:38
  714.1 40.3 %psum.7 = f32[8,8]{0,1:T(8,128)S(1)} all-reduce(f32[8,8]{0,1:T(8,128)S(1)} %fusion.15), channel_id=1, replica_groups=mesh['state'=4,'basis'=8] {'state','basis'}, use_global_device_ids=true, to_apply=%region_0.0 | all-reduce | flops 64 | bytes 512 | tf_op jit(solution)/shard_map/psum | solution.py:39
  754.5 0.1 copy.47
  754.5 0.7 cholesky.17
  755.3 0.7 compare_reduce_fusion
  756.0 0.7 fusion.12
  756.7 0.6 custom-call.6
  757.3 0.2 convolution_bitcast_fusion.3
  757.5 7.5 dot_general.32
  765.0 7.8 fusion.2
  772.8 2.4 copy.50
  775.3 95.5 %all_to_all.70 = f32[8,64,2000]{2,1,0:T(8,128)S(1)} all-to-all(f32[8,64,2000]{2,1,0:T(8,128)S(1)} %copy.50), channel_id=1, replica_groups=mesh['state'=4,'basis'=8] {'state'}, dimensions={0} | all-to-all | bytes 8192000 | tf_op jit(solution)/shard_map/all_to_all | solution.py:46
  870.8 4.6 copy.65
  875.4 6.3 all_to_all.60
  881.7 5.4 copy.52
  887.1 51.7 %all_to_all.71 = f32[2,64,8000]{2,0,1:T(2,128)S(1)} all-to-all(f32[2,64,8000]{2,0,1:T(2,128)S(1)} %copy.52), channel_id=1, replica_groups=mesh['state'=4,'basis'=8] {'basis'}, dimensions={1} | all-to-all | bytes 8192000 | tf_op jit(solution)/shard_map/all_to_all | solution.py:45
  938.8 0.3 copy.66
  939.1 0.0 copy-start.1
  939.1 2.7 copy.54
  941.8 4.2 all_to_all.64
  946.1 0.0 copy-done.1
  (3 shorter events, 0.1 us)
Async XLA Ops:
  0.0 479.7 %copy-start = (f32[64,64]{1,0:T(8,128)S(1)}, f32[64,64]{1,0:T(8,128)}, u32[]{:S(2)}) copy-start(f32[64,64]{1,0:T(8,128)} %param.9) | copy-start | bytes 49156
  0.0 4.5 copy-start.3
  198.8 5.3 copy-start.6
  198.8 53.5 %all-to-all-start = ((f32[8,1,128000]{2,1,0:T(1,128)}), f32[8,1,128000]{2,1,0:T(1,128)}, u32[]{:S(2)}, u32[]{:S(2)}) async-start(f32[8,1,128000]{2,1,0:T(1,128)} %reshape.39), calls=%async_computation | async-start | bytes 8192000 | tf_op jit(solution)/shard_map/all_to_all | solution.py:22
  494.5 8.8 copy-start.4
  503.3 6.6 copy-start.5
  517.0 8.2 copy-start.2
  939.1 7.0 copy-start.1
where the time goes:
time: 958 us; the launch traced here: 946 us
  local copies, waits for them, and re-layouts  516 us (54%)
  blocking collectives  282 us (29%)
  matrix products  63.6 us (7%)
  waiting for transfers between devices  48.1 us (5%)
  other arithmetic  30.9 us (3%)
    unnamed x19, local copies, waits for them, and re-layouts  303 us
    all_to_all x1, blocking collectives, body(): lax.all_to_all(local_result, 'state', split_axis=0, concat_axis=2, tiled=...  95.5 us
    all_to_all x1, blocking collectives, body(): lax.all_to_all(stepped, 'state', split_axis=2, concat_axis=0, tiled=True)  94.7 us
    all_to_all x2, local copies, waits for them, and re-layouts, body(): lax.all_to_all(head, 'basis', split_axis=2, concat_axis=1, tiled=True)  71.6 us
    all_to_all x1, blocking collectives, body(): lax.all_to_all(lax.all_to_all(local_result, 'state', split_axis=0, concat...  51.7 us
    reshape x1, local copies, waits for them, and re-layouts, body(): head = head.reshape(panel_size, level_count, joint)  49.2 us
    all_to_all x1, waiting for transfers between devices, body(): lax.all_to_all(head, 'basis', split_axis=2, concat_axis=1, tiled=True)  48.1 us
    psum x1, blocking collectives, body(): gram = lax.psum(partial_gram, ('state', 'basis')) / basis_total  40.3 us
  transfers between devices with their start and end apart: 1, of which 1 were waited for; matrix products, arithmetic and copies ran while one was open for 0% of the time, Pallas kernels for 0%

commit v1 on v0

--- a/solution.py
+++ b/solution.py
@@ -19,7 +19,10 @@
         precision=highest,
     )
     head = head.reshape(panel_size, level_count, joint)
-    panel_block = lax.all_to_all(head, "basis", split_axis=2, concat_axis=1, tiled=True)
+    panel_block = jnp.concatenate(
+        lax.all_to_all(jnp.stack(jnp.split(head, lax.axis_size("basis"), axis=2)), "basis", 0, 0),
+        axis=1,
+    )
     items, cavity_all, columns = panel_block.shape
     grid = jnp.einsum("qc,kcr->kqr", cavity_forward, panel_block, precision=highest)
     grid = jnp.einsum(

time: 958 us -> 556 us (0.58)
  local copies, waits for them, and re-layouts: 516 us -> 132 us
  other arithmetic: 30.9 us -> 17.2 us
    unnamed x19 -> x26, local copies, waits for them, and re-layouts: 303 us -> 33.6 us
    all_to_all x2 -> x0, local copies, waits for them, and re-layouts: 71.6 us -> none  [body(): lax.all_to_all(head, 'basis', split_axis=2, concat_axis=1, tiled=True)]
    reshape x1, local copies, waits for them, and re-layouts: 49.2 us -> 4.25 us  [body(): head = head.reshape(panel_size, level_count, joint)]
    all_to_all x1 -> x0, other arithmetic: 13.6 us -> none  [body(): lax.all_to_all(head, 'basis', split_axis=2, concat_axis=1, tiled=True)]
where the time goes in v1:
time: 556 us; the launch traced here: 550 us
  blocking collectives  282 us (51%)
  local copies, waits for them, and re-layouts  132 us (24%)
  matrix products  63.5 us (11%)
  waiting for transfers between devices  48.3 us (9%)
  other arithmetic  17.2 us (3%)
  starting transfers between devices  5.85 us (1%)
    all_to_all x1, blocking collectives, body(): lax.all_to_all(local_result, 'state', split_axis=0, concat_axis=2, tiled=...  95.5 us
    all_to_all x1, blocking collectives, body(): lax.all_to_all(stepped, 'state', split_axis=2, concat_axis=0, tiled=True)  94.9 us
    all_to_all x1, blocking collectives, body(): lax.all_to_all(lax.all_to_all(local_result, 'state', split_axis=0, concat...  51.7 us
    all_to_all x1, waiting for transfers between devices, body(): lax.all_to_all(jnp.stack(jnp.split(head, lax.axis_size('basis'), axis=2))...  48.3 us
    psum x1, blocking collectives, body(): gram = lax.psum(partial_gram, ('state', 'basis')) / basis_total  40.3 us
    unnamed x26, local copies, waits for them, and re-layouts  33.6 us
    all_to_all x3, local copies, waits for them, and re-layouts, body(): lax.all_to_all(local_result, 'state', split_axis=0, concat_axis=2, tiled=...  16.3 us
    all_to_all x1, other arithmetic, body(): lax.all_to_all(stepped, 'state', split_axis=2, concat_axis=0, tiled=True)  14.4 us
  transfers between devices with their start and end apart: 1, of which 1 were waited for; matrix products, arithmetic and copies ran while one was open for 0% of the time, Pallas kernels for 0%

profile of v1, /device:TPU:0, one launch (start us, length us, event | category | flops | bytes accessed | tf_op | source)
XLA Modules:
  0.0 549.6 jit_solution(4596116572299702639)
XLA Ops:
  0.0 0.0 copy-start
  0.0 0.0 copy-start.4
  0.0 4.5 reshape.34
  4.5 0.0 copy-done.4
  4.5 7.9 %convolution_bitcast_fusion.2 = f32[2,8,40,1600]{3,2,1,0:T(8,128)} fusion(f32[2,8,40,1600]{3,2,1,0:T(8,128)} %reshape.34, f32[40,40]{1,0:T(8,128)S(1)} %copy-done.4), kind=kOutput, calls=%fused_computation.10 | convolution fusion | flops 491520000 | bytes 8198400 | tf_op jit(solution)/shard_map/ab,scbr->scar/dot_general | solution.py:15
  12.4 4.3 reshape.35
  16.7 0.0 copy-start.2
  16.7 2.0 fusion.14
  18.7 2.0 fusion.13
  20.7 1.9 fusion.12
  22.6 2.0 fusion.11
  24.6 0.0 copy-done.2
  24.6 0.8 fusion.10
  25.5 1.0 fusion.9
  26.5 0.8 fusion.8
  27.3 1.0 fusion.7
  28.3 0.0 copy-start.7
  28.3 5.8 %all-to-all-start = ((f32[8,2,8,8000]{3,2,1,0:T(8,128)}), f32[8,2,8,8000]{3,2,1,0:T(8,128)}, u32[]{:S(2)}, u32[]{:S(2)}) async-start(f32[8,2,8,8000]{3,2,1,0:T(8,128)} %fusion.7), calls=%async_computation | async-start | bytes 8257536 | tf_op jit(solution)/shard_map/all_to_all | solution.py:23
  34.1 0.0 copy-done.7
  34.1 0.1 copy.40
  34.2 48.3 %all-to-all-done = f32[8,2,8,8000]{3,2,1,0:T(8,128)} async-done(((f32[8,2,8,8000]{3,2,1,0:T(8,128)}), f32[8,2,8,8000]{3,2,1,0:T(8,128)}, u32[]{:S(2)}, u32[]{:S(2)}) %all-to-all-start) | async-done | bytes 4096032 | tf_op jit(solution)/shard_map/all_to_all | solution.py:23
  82.6 0.0 copy-done
  82.6 8.0 %convolution_bitcast_fusion.1 = f32[2,64,8000]{2,1,0:T(8,128)} fusion(f32[64,64]{1,0:T(8,128)S(1)} %copy-done, f32[8,2,8,8000]{3,2,1,0:T(8,128)} %all-to-all-done), kind=kOutput, calls=%fused_computation.1 | convolution fusion | flops 786432000 | bytes 8208384 | tf_op jit(solution)/shard_map/qc,kcr->kqr/dot_general | solution.py:27
  90.6 6.8 %copy.38 = f32[2,64,8000]{1,2,0:T(8,128)} copy(f32[2,64,8000]{2,1,0:T(8,128)} %convolution_bitcast_fusion.1) | data formatting | bytes 8192000 | tf_op jit(solution)/shard_map/qc,kcr->kqr/transpose | solution.py:27
  97.4 0.0 copy-start.5
  97.4 8.8 %copy.39 = f32[2,64,200,40]{2,3,1,0:T(8,128)} copy(f32[2,64,200,40]{1,3,2,0:T(8,128)} %bitcast.110) | data formatting | bytes 8192000 | tf_op jit(solution)/shard_map/reshape | solution.py:30
  106.2 0.0 copy-done.5
  106.2 0.0 copy-start.6
  106.2 6.5 %fusion.18 = f32[2,64,200,40]{2,3,1,0:T(8,128)S(1)} fusion(f32[2,64,200,40]{2,3,1,0:T(8,128)} %copy.39, f32[40,40]{1,0:T(8,128)S(1)} %copy-done.5), kind=kOutput, calls=%fused_computation.32 | convolution fusion | flops 491520000 | bytes 8198400 | tf_op jit(solution)/shard_map/kqtm,nm->kqtn/dot_general | solution.py:28
  112.7 0.0 copy-done.6
  112.7 7.0 %fusion = f32[2,64,200,40]{2,3,1,0:T(8,128)} fusion(f32[2,64,200,40]{2,3,1,0:T(8,128)S(1)} %fusion.18, f32[64,40]{1,0:T(8,128)S(1)} %copy.40, f32[40,40]{1,0:T(8,128)S(1)} %copy-done.6), kind=kOutput, calls=%fused_computation.2 | convolution fusion | flops 492544000 | bytes 8208640 | tf_op jit(solution)/shard_map/kqtn,mn->kqtm/dot_general | solution.py:35
  119.7 0.0 copy-start.3
  119.7 8.4 %copy.41 = f32[2,64,200,40]{1,3,2,0:T(8,128)} copy(f32[2,64,200,40]{2,3,1,0:T(8,128)} %fusion) | data formatting | bytes 8192000 | tf_op jit(solution)/shard_map/kqtn,mn->kqtm/dot_general | solution.py:35
  128.1 0.0 copy-done.3
  128.1 13.7 %convolution_bitcast_fusion = f32[2,64,8000]{2,1,0:T(8,128)} fusion(f32[2,64,8000]{1,2,0:T(8,128)} %bitcast.108, f32[64,64]{1,0:T(8,128)S(1)} %copy-done.3), kind=kOutput, calls=%fused_computation | convolution fusion | flops 786432000 | bytes 8208384 | tf_op jit(solution)/shard_map/cq,kqr->kcr/dot_general | solution.py:37
  141.8 10.7 %copy.43 = f32[2,64,8000]{1,0,2:T(2,128)} copy(f32[2,64,8000]{2,1,0:T(8,128)} %convolution_bitcast_fusion) | data formatting | bytes 8192000 | tf_op jit(solution)/shard_map/cq,kqr->kcr/transpose | solution.py:37
  152.5 11.1 %reshape.47 = f32[4,1,256000]{2,1,0:T(1,128)} reshape(f32[8000,2,64]{2,1,0:T(2,128)} %bitcast.111) | data formatting | bytes 8192000
  163.6 94.9 %all_to_all.56 = f32[4,1,256000]{2,1,0:T(1,128)} all-to-all(f32[4,1,256000]{2,1,0:T(1,128)} %reshape.47), channel_id=1, replica_groups=mesh['state'=4,'basis'=8] {'state'}, dimensions={0} | all-to-all | bytes 8192000 | tf_op jit(solution)/shard_map/all_to_all | solution.py:38
  258.5 0.5 broadcast.49
  259.0 14.4 %reduce.6 = f32[4,256000]{1,0:T(4,128)} reduce(f32[4,1,256000]{2,1,0:T(1,128)} %all_to_all.56, f32[]{:T(128)} %broadcast.49), dimensions={1}, to_apply=%all_to_all.41.reduce_sub_computation | reduce | bytes 8192004 | tf_op jit(solution)/shard_map/all_to_all | solution.py:38
  273.4 11.7 %reshape.48 = f32[8000,2,64]{2,1,0:T(2,128)} reshape(f32[4,256000]{1,0:T(4,128)} %reduce.6) | data formatting | bytes 8192000
  285.1 12.6 %copy.44 = f32[2,64,4,2000]{3,1,0,2:T(8,128)} copy(f32[2,64,4,2000]{1,0,3,2:T(2,128)} %bitcast.112) | data formatting | bytes 8192000 | tf_op jit(solution)/shard_map/all_to_all | solution.py:38
  297.6 7.5 %reshape.40 = f32[8,128000]{1,0:T(8,128)} reshape(f32[4,2,64,2000]{3,2,1,0:T(8,128)} %bitcast.113) | data formatting | bytes 8192000 | tf_op jit(solution)/shard_map/reshape | solution.py:40
  305.1 12.3 %fusion.24 = f32[8,8]{0,1:T(8,128)S(1)} fusion(f32[8,128000]{1,0:T(8,128)} %reshape.40), kind=kOutput, calls=%fused_computation.45 | convolution fusion | flops 98304000 | bytes 4096256 | tf_op jit(solution)/shard_map/dot_general | solution.py:41
  317.5 40.3 %psum.7 = f32[8,8]{0,1:T(8,128)S(1)} all-reduce(f32[8,8]{0,1:T(8,128)S(1)} %fusion.24), channel_id=1, replica_groups=mesh['state'=4,'basis'=8] {'state','basis'}, use_global_device_ids=true, to_apply=%region_0.0 | all-reduce | flops 64 | bytes 512 | tf_op jit(solution)/shard_map/psum | solution.py:42
  357.8 0.1 copy.46
  357.9 0.7 cholesky.17
  358.6 0.7 compare_reduce_fusion
  359.3 0.7 fusion.21
  360.0 0.6 custom-call.6
  360.7 0.2 convolution_bitcast_fusion.3
  360.8 7.5 %dot_general.32 = f32[64,2000,8]{1,0,2:T(8,128)} reshape(f32[128000,8]{0,1:T(8,128)} %bitcast.109) | data formatting | bytes 8192000 | tf_op jit(solution)/shard_map/dot_general | solution.py:46
  368.3 7.8 %fusion.2 = f32[8,64,2000]{2,0,1:T(8,128)S(1)} fusion(f32[8,8,1]{1,0,2:T(8,128)S(1)} %convolution_bitcast_fusion.3, f32[64,2000,8]{1,0,2:T(8,128)} %dot_general.32), kind=kOutput, calls=%fused_computation.5 | convolution fusion | flops 98304000 | bytes 8192256 | tf_op jit(solution)/shard_map/dot_general | solution.py:46
  376.2 2.4 copy.49
  378.6 95.5 %all_to_all.57 = f32[8,64,2000]{2,1,0:T(8,128)S(1)} all-to-all(f32[8,64,2000]{2,1,0:T(8,128)S(1)} %copy.49), channel_id=1, replica_groups=mesh['state'=4,'basis'=8] {'state'}, dimensions={0} | all-to-all | bytes 8192000 | tf_op jit(solution)/shard_map/all_to_all | solution.py:49
  474.1 4.6 copy.67
  478.7 6.3 %all_to_all.47 = f32[2,64,8000]{2,1,0:T(8,128)} reshape(f32[2,64,4,2000]{3,2,1,0:T(4,128)} %bitcast.115) | data formatting | bytes 8192000 | tf_op jit(solution)/shard_map/all_to_all | solution.py:49
  485.1 5.4 copy.51
  490.4 51.7 %all_to_all.58 = f32[2,64,8000]{2,0,1:T(2,128)S(1)} all-to-all(f32[2,64,8000]{2,0,1:T(2,128)S(1)} %copy.51), channel_id=1, replica_groups=mesh['state'=4,'basis'=8] {'basis'}, dimensions={1} | all-to-all | bytes 8192000 | tf_op jit(solution)/shard_map/all_to_all | solution.py:48
  542.1 0.3 copy.68
  542.4 0.0 copy-start.1
  542.4 2.7 copy.53
  545.1 4.2 all_to_all.51
  549.4 0.0 copy-done.1
  (3 shorter events, 0.1 us)
Async XLA Ops:
  0.0 82.6 %copy-start = (f32[64,64]{1,0:T(8,128)S(1)}, f32[64,64]{1,0:T(8,128)}, u32[]{:S(2)}) copy-start(f32[64,64]{1,0:T(8,128)} %param.9) | copy-start | bytes 49156
  0.0 4.5 copy-start.4
  16.7 8.0 %copy-start.2 = (f32[2,8,64000]{2,1,0:T(8,128)S(1)}, f32[2,8,64000]{2,1,0:T(8,128)}, u32[]{:S(2)}) copy-start(f32[2,8,64000]{2,1,0:T(8,128)} %reshape.35) | copy-start | bytes 12288004
  28.3 5.9 %copy-start.7 = (f32[64,40]{0,1:T(8,128)S(1)}, f32[64,40]{0,1:T(8,128)}, u32[]{:S(2)}) copy-start(f32[64,40]{0,1:T(8,128)} %param.10) | copy-start | bytes 30724
  28.3 54.3 %all-to-all-start = ((f32[8,2,8,8000]{3,2,1,0:T(8,128)}), f32[8,2,8,8000]{3,2,1,0:T(8,128)}, u32[]{:S(2)}, u32[]{:S(2)}) async-start(f32[8,2,8,8000]{3,2,1,0:T(8,128)} %fusion.7), calls=%async_computation | async-start | bytes 8257536 | tf_op jit(solution)/shard_map/all_to_all | solution.py:23
  97.4 8.8 %copy-start.5 = (f32[40,40]{1,0:T(8,128)S(1)}, f32[40,40]{1,0:T(8,128)}, u32[]{:S(2)}) copy-start(f32[40,40]{1,0:T(8,128)} %param.11) | copy-start | bytes 19204
  106.2 6.6 %copy-start.6 = (f32[40,40]{1,0:T(8,128)S(1)}, f32[40,40]{1,0:T(8,128)}, u32[]{:S(2)}) copy-start(f32[40,40]{1,0:T(8,128)} %param.13) | copy-start | bytes 19204
  119.7 8.4 %copy-start.3 = (f32[64,64]{1,0:T(8,128)S(1)}, f32[64,64]{1,0:T(8,128)}, u32[]{:S(2)}) copy-start(f32[64,64]{1,0:T(8,128)} %param.12) | copy-start | bytes 49156
  542.4 7.0 %copy-start.1 = (f32[64,64]{1,0:T(8,128)S(1)}, f32[64,64]{1,0:T(8,128)}, u32[]{:S(2)}) copy-start(f32[64,64]{1,0:T(8,128)} %param.9) | copy-start | bytes 49156
